TPU v7x, 128 devices: a whole 4x4x4 slice. The times are simulated.
128 devices in a mesh: ctx: 16 (over z, x_lo, core), tp: 8 (over y, x_hi).
Axes of the slice: x: 4 (x_hi: 2, x_lo: 2; x = x_hi * 2 + x_lo), y: 4, z: 4, core: 2. Of those that a mesh axis runs over, the one named last changes fastest.
Arguments:
- projected: bfloat16 [3, 4096, 8192], P(None, 'ctx', 'tp'), may hold values from -6 to 6
- short_taps: float32 [3, 7, 8192], P(None, None, 'tp'), may hold values from -2.4 to 2.4
- range_filter: bfloat16 [64, 1024], P('tp'), may hold values from -0.1875 to 0.1875
- skip_gain: float32 [8192], P('tp'), may hold values from -4 to 4
- out_weight: bfloat16 [8192, 8192], P('ctx', 'tp'), may hold values from -0.0625 to 0.0625
Outputs:
- mixed: bfloat16 [4096, 8192], P('ctx', 'tp')
All inputs are finite; a program needn't handle non-finite values.
Results may differ from a plain program's by a relative error of at most 0.0057.
Values may be sent and summed in bfloat16 or wider, within the bound.
A program may use at most 192 MiB of HBM per device.

v0:
```python
import jax
import jax.numpy as jnp
from jax import lax
from jax.sharding import PartitionSpec as P


def passed_along(block, axis, distance):
    devices = range(lax.axis_size(axis))
    route = [((i - distance) % len(devices), i) for i in devices]
    return lax.ppermute(block, axis, route)


def short_conv(extended, tap_rows, length):
    accumulated = jnp.zeros((length, extended.shape[1]), jnp.float32)
    rim_width = tap_rows.shape[0] - 1
    for lag_index in range(tap_rows.shape[0]):
        window = extended[rim_width - lag_index : rim_width - lag_index + length]
        accumulated = accumulated + tap_rows[lag_index][None, :] * window.astype(jnp.float32)
    return accumulated


def toeplitz_slabs(range_filter, length, span_blocks):
    kept = range_filter.shape[1]
    offsets = lax.broadcasted_iota(jnp.int32, (span_blocks + 1, length, length), 0)
    rows_at = lax.broadcasted_iota(jnp.int32, (span_blocks + 1, length, length), 1)
    cols_at = lax.broadcasted_iota(jnp.int32, (span_blocks + 1, length, length), 2)
    lag_at = offsets * length + rows_at - cols_at
    inside = jnp.logical_and(lag_at >= 0, lag_at < kept)
    clipped = jnp.clip(lag_at, 0, kept - 1)
    looked = jnp.take(range_filter, clipped.reshape(-1), axis=1).reshape(
        range_filter.shape[0], span_blocks + 1, length, length
    )
    return jnp.where(inside[None], looked, jnp.zeros((), range_filter.dtype))


def local(projected, short_taps, range_filter, skip_gain, out_weight):
    length = projected.shape[1]
    width_dev = projected.shape[2]
    groups = range_filter.shape[0]
    group_width = width_dev // groups
    rim_width = short_taps.shape[1] - 1
    span_blocks = range_filter.shape[1] // length
    rim_block = passed_along(projected[:, length - rim_width :, :], "ctx", 1)
    extended = jnp.concatenate([rim_block, projected], axis=1)
    query_feat = short_conv(extended[0], short_taps[0], length)
    key_feat = short_conv(extended[1], short_taps[1], length)
    value_feat = short_conv(extended[2], short_taps[2], length)
    mixed_in = (key_feat * value_feat).astype(jnp.bfloat16)
    slabs = toeplitz_slabs(range_filter, length, span_blocks)

    def correlate(arrived, offset):
        grouped = arrived.reshape(length, groups, group_width)
        product = jnp.einsum(
            "gam,mgc->agc", slabs[:, offset], grouped, preferred_element_type=jnp.float32
        )
        return product.reshape(length, width_dev)

    toeplitz = correlate(mixed_in, 0)
    for offset in range(1, span_blocks + 1):
        arrived = passed_along(mixed_in, "ctx", offset)
        toeplitz = toeplitz + correlate(arrived, offset)
    restored = lax.optimization_barrier(mixed_in).astype(jnp.float32)
    gated_out = (query_feat * (toeplitz + skip_gain[None, :] * restored)).astype(jnp.bfloat16)
    gathered = lax.all_gather(gated_out, "tp", axis=1, tiled=True)
    summed = jnp.dot(
        gathered,
        lax.all_gather(out_weight, "ctx", axis=0, tiled=True),
        preferred_element_type=jnp.float32,
    )
    return summed.astype(jnp.bfloat16)


def solution(mesh):
    placed = (P(None, "ctx", "tp"), P(None, None, "tp"), P("tp", None), P("tp"), P("ctx", "tp"))
    return jax.shard_map(
        local, mesh=mesh, in_specs=placed, out_specs=P("ctx", "tp"), check_vma=False
    )
```

profile of v0, /device:TPU:1, one launch (start us, length us, event | category | flops | bytes accessed | tf_op | source)
XLA Modules:
  0.0 1476.2 jit_solution(5024653289956213897)
XLA Ops:
  6.5 1.5 slice.240
  8.0 2.6 collective-permute-start
  10.6 0.3 fusion.2
  10.9 1.0 fusion.5
  11.9 0.7 fusion.67
  12.8 1.3 min.14
  14.1 1.4 compare_select_fusion
  15.7 1133.3 %gather_fusion = bf16[327680,8]{1,0:T(8,128)(2,1)} fusion(bf16[8,1024]{0,1:T(8,128)(2,1)S(1)} %copy.40, s32[327680]{0:T(1024)S(1)} %broadcast_clamp_fusion), kind=kCustom, calls=%fused_computation | custom fusion | bytes 11796480 | tf_op jit(solution)/shard_map/jit(_take)/gather | solution.py:30
  1149.1 60.1 %copy.42 = bf16[8,5,256,256]{3,2,0,1:T(8,128)(2,1)} copy(bf16[8,5,256,256]{0,3,2,1:T(8,128)(2,1)} %bitcast.44) | data formatting | bytes 10485760 | tf_op jit(solution)/shard_map/jit(_take)/gather | solution.py:30
  1209.2 6.1 select_select_fusion
  1215.4 0.8 fusion.68
  1216.3 3.8 fusion.19
  1220.1 1.7 collective-permute-start.4
  1221.8 0.7 collective-permute-start.3
  1222.5 2.4 collective-permute-start.1
  1224.9 1.3 collective-permute-start.2
  1226.2 1.3 copy.61
  1227.5 3.4 fusion.58
  1230.9 2.5 copy.60
  1233.5 2.5 copy.59
  1236.0 2.5 copy.58
  1238.6 2.6 copy.57
  1241.1 1.3 copy.56
  1242.4 3.9 fusion.46
  1246.4 2.6 copy.55
  1249.0 2.5 copy.54
  1251.5 2.5 copy.53
  1254.0 2.5 copy.52
  1256.6 2.6 copy.51
  1259.2 2.5 copy.50
  1261.7 1.3 copy.49
  1263.0 2.6 copy.48
  1265.7 7.1 fusion.8
  1272.8 1.0 copy.46
  1273.8 1.2 copy.45
  1275.1 2.9 fusion.6
  1278.0 2.1 copy.43
  1280.0 2.7 fusion.7
  1282.7 2.7 convolution_add_fusion.1
  1285.4 1.3 copy.44
  1286.8 3.3 fusion.1
  1290.2 1.6 copy.47
  1291.8 3.0 fusion.11
  1294.8 0.3 all-gather.5.cloned.1.call-start
  1295.1 0.5 all-gather.5.cloned.1.call-update
  1295.6 69.1 %all-gather.3.cloned.1.call-done = bf16[256,8192]{1,0:T(8,128)(2,1)} async-done(((bf16[256,1024]{1,0:T(8,128)(2,1)}), bf16[256,8192]{1,0:T(8,128)(2,1)}) %all-gather.3.cloned.1.call-update) | async-done | bytes 4194320 | tf_op jit(solution)/shard_map/all_gather | solution.py:64
  1364.7 92.4 %all-gather.5.cloned.1.call-done = bf16[8192,1024]{1,0:T(8,128)(2,1)} async-done(((bf16[512,1024]{1,0:T(8,128)(2,1)}), bf16[8192,1024]{1,0:T(8,128)(2,1)}) %all-gather.5.cloned.1.call-update) | async-done | bytes 16777232 | tf_op jit(solution)/shard_map/all_gather | solution.py:67
  1457.1 12.3 convolution_convert_fusion
  (68 shorter events, 0.5 us)
Async XLA Ops:
  6.5 5.4 copy-start.3
  6.5 6.1 copy-start.20
  6.5 1358.2 %all-gather.3.cloned.1.call-start = ((), (), s32[]{:S(2)}) async-start(), calls=%async_computation | async-start | bytes 4718592 | tf_op jit(solution)/shard_map/all_gather | solution.py:64
  8.0 1208.2 %collective-permute-start = (bf16[3,6,1024]{2,1,0:T(8,128)(2,1)}, bf16[3,6,1024]{2,1,0:T(8,128)(2,1)}, u32[]{:S(2)}, u32[]{:S(2)}) collective-permute-start(bf16[3,6,1024]{2,1,0:T(8,128)(2,1)} %slice.240), channel_id=1, source_target_pairs={{120,0},{0,8},{8,16},{16,24},{24,32},{32,40},{40,48},{48,56},{56,6... | collective-permute-start | bytes 110600 | tf_op jit(solution)/shard_map/ppermute | solution.py:10
  1209.1 7.1 copy-start
  1209.2 7.1 copy-start.4
  1209.2 7.1 copy-start.6
  1209.2 7.1 copy-start.8
  1209.2 7.1 copy-start.10
  1209.2 7.1 copy-start.12
  1209.2 7.1 copy-start.14
  1209.2 7.1 copy-start.16
  1209.2 7.1 copy-start.18
  1220.1 52.7 %collective-permute-start.4 = (bf16[256,1024]{1,0:T(8,128)(2,1)}, bf16[256,1024]{1,0:T(8,128)(2,1)S(1)}, u32[]{:S(2)}, u32[]{:S(2)}) collective-permute-start(bf16[256,1024]{1,0:T(8,128)(2,1)} %get-tuple-element.5), channel_id=1, source_target_pairs={{96,0},{104,8},{112,16},{120,24},{0,32},{8,40},{16,48},{24,56},{32... | collective-permute-start | bytes 1572872 | tf_op jit(solution)/shard_map/ppermute | solution.py:10
  1221.8 52.0 %collective-permute-start.3 = (bf16[256,1024]{1,0:T(8,128)(2,1)}, bf16[256,1024]{1,0:T(8,128)(2,1)}, u32[]{:S(2)}, u32[]{:S(2)}) collective-permute-start(bf16[256,1024]{1,0:T(8,128)(2,1)} %get-tuple-element.5), channel_id=1, source_target_pairs={{104,0},{112,8},{120,16},{0,24},{8,32},{16,40},{24,48},{32,56},{40... | collective-permute-start | bytes 1572872 | tf_op jit(solution)/shard_map/ppermute | solution.py:10
  1222.5 55.4 %collective-permute-start.1 = (bf16[256,1024]{1,0:T(8,128)(2,1)}, bf16[256,1024]{1,0:T(8,128)(2,1)}, u32[]{:S(2)}, u32[]{:S(2)}) collective-permute-start(bf16[256,1024]{1,0:T(8,128)(2,1)} %get-tuple-element.5), channel_id=1, source_target_pairs={{120,0},{0,8},{8,16},{16,24},{24,32},{32,40},{40,48},{48,56},{56,6... | collective-permute-start | bytes 1572872 | tf_op jit(solution)/shard_map/ppermute | solution.py:10
  1224.9 60.5 %collective-permute-start.2 = (bf16[256,1024]{1,0:T(8,128)(2,1)}, bf16[256,1024]{1,0:T(8,128)(2,1)}, u32[]{:S(2)}, u32[]{:S(2)}) collective-permute-start(bf16[256,1024]{1,0:T(8,128)(2,1)} %get-tuple-element.5), channel_id=1, source_target_pairs={{112,0},{120,8},{0,16},{8,24},{16,32},{24,40},{32,48},{40,56},{48,... | collective-permute-start | bytes 1572872 | tf_op jit(solution)/shard_map/ppermute | solution.py:10
  1261.7 3.9 copy-start.5
  1261.7 3.9 copy-start.7
  1261.7 3.9 copy-start.9
  1261.7 3.9 copy-start.11
  1261.7 3.9 copy-start.13
  1261.7 3.9 copy-start.15
  1261.7 3.9 copy-start.17
  1261.7 3.9 copy-start.19
  1280.0 2.7 copy-start.2
  1285.4 1.4 copy-start.1
  1290.1 1.6 copy-start.21
  1290.1 1.6 copy-start.22
  1290.1 1.6 copy-start.23
  1290.2 1.6 copy-start.24
  1290.2 1.7 copy-start.25
  1290.2 1.7 copy-start.26
  1290.2 1.7 copy-start.27
  1290.2 1.7 copy-start.28
  1294.8 162.2 %all-gather.5.cloned.1.call-start = ((), (), s32[]{:S(2)}) async-start(), calls=%async_computation.1 | async-start | bytes 17825792 | tf_op jit(solution)/shard_map/all_gather | solution.py:67
Sparse Core Ops, SparseCore 0:
  1295.0 69.6 all-gather.2
  1366.4 90.6 all-gather.4
where the time goes:
time: 1480 us
  local copies, waits for them, and re-layouts  1240 us (84%)
  waiting for transfers between devices  162 us (11%)
  matrix products  31.1 us (2%)
  other arithmetic  23.1 us (2%)
    gather x2, local copies, waits for them, and re-layouts, toeplitz_slabs(): jnp.take(range_filter, clipped.reshape(-1), axis=1)  1190 us
    all_gather x1, waiting for transfers between devices, local(): lax.all_gather(out_weight, 'ctx', axis=0, tiled=True)  92.4 us
    all_gather x1, waiting for transfers between devices, local(): gathered = lax.all_gather(gated_out, 'tp', axis=1, tiled=True)  69.1 us
    convert_element_type x14, local copies, waits for them, and re-layouts, short_conv(): window.astype(jnp.float32)  32 us
  transfers between devices with their start and end apart: 7, of which 2 were waited for; matrix products, arithmetic and copies ran while one was open for 86% of the time, Pallas kernels for 0%

commit v1 on v0

--- a/solution.py
+++ b/solution.py
@@ -2,6 +2,7 @@
 import jax.numpy as jnp
 from jax import lax
 from jax.sharding import PartitionSpec as P
+from jax.lax import all_to_all, axis_size
 
 
 def passed_along(block, axis, distance):
@@ -61,7 +62,14 @@
         toeplitz = toeplitz + correlate(arrived, offset)
     restored = lax.optimization_barrier(mixed_in).astype(jnp.float32)
     gated_out = (query_feat * (toeplitz + skip_gain[None, :] * restored)).astype(jnp.bfloat16)
-    gathered = lax.all_gather(gated_out, "tp", axis=1, tiled=True)
+
+    def match_panels(local_values, row_axis):
+        big = jnp.concatenate(
+            all_to_all(jnp.stack(axis_size(row_axis) * [local_values]), row_axis, 0, 0), 1
+        )
+        return big
+
+    gathered = match_panels(gated_out, "tp")
     summed = jnp.dot(
         gathered,
         lax.all_gather(out_weight, "ctx", axis=0, tiled=True),

time: 1480 us -> 1370 us (0.926)
  waiting for transfers between devices: 162 us -> 0.03 us
  blocking collectives: 0 us -> 57.3 us
    all_gather x1, waiting for transfers between devices: 92.4 us -> 0.01 us  [local(): lax.all_gather(out_weight, 'ctx', axis=0, tiled=True)]
    all_gather x1 -> x0, waiting for transfers between devices: 69.1 us -> none  [local(): gathered = lax.all_gather(gated_out, 'tp', axis=1, tiled=True)]
    all_to_all x0 -> x1, blocking collectives: none -> 57.3 us  [match_panels(): all_to_all(jnp.stack(axis_size(row_axis) * [local_values]), row_axis, 0, 0)]
  transfers between devices with their start and end apart: 7 -> 6, of which waited for: 2 -> 0; matrix products, arithmetic and copies ran while one was open for 86% -> 93% of each run, Pallas kernels for 0% -> 0%
where the time goes in v1:
time: 1370 us
  local copies, waits for them, and re-layouts  1250 us (91%)
  blocking collectives  57.3 us (4%)
  matrix products  27.4 us (2%)
  other arithmetic  19.2 us (1%)
    gather x2, local copies, waits for them, and re-layouts, toeplitz_slabs(): jnp.take(range_filter, clipped.reshape(-1), axis=1)  1200 us
    all_to_all x1, blocking collectives, match_panels(): all_to_all(jnp.stack(axis_size(row_axis) * [local_values]), row_axis, 0, 0)  57.3 us
    convert_element_type x14, local copies, waits for them, and re-layouts, short_conv(): window.astype(jnp.float32)  32.2 us
  transfers between devices with their start and end apart: 6, of which 0 were waited for; matrix products, arithmetic and copies ran while one was open for 93% of the time, Pallas kernels for 0%

profile of v1, /device:TPU:1, one launch (start us, length us, event | category | flops | bytes accessed | tf_op | source)
XLA Modules:
  0.0 1371.7 jit_solution(13394615820131813043)
XLA Ops:
  6.5 0.8 slice.240
  7.4 2.7 collective-permute-start
  10.0 0.3 fusion.2
  10.4 1.3 min.14
  11.7 1.4 compare_select_fusion
  13.2 0.2 copy.40
  13.3 0.2 broadcast_clamp_fusion
  13.5 1141.3 %gather_fusion = bf16[327680,8]{1,0:T(8,128)(2,1)} fusion(bf16[8,1024]{0,1:T(8,128)(2,1)S(1)} %copy.40, s32[327680]{0:T(1024)S(1)} %broadcast_clamp_fusion), kind=kCustom, calls=%fused_computation | custom fusion | bytes 11796480 | tf_op jit(solution)/shard_map/jit(_take)/gather | solution.py:31
  1154.9 60.1 %copy.42 = bf16[8,5,256,256]{3,2,0,1:T(8,128)(2,1)} copy(bf16[8,5,256,256]{0,3,2,1:T(8,128)(2,1)} %bitcast.44) | data formatting | bytes 10485760 | tf_op jit(solution)/shard_map/jit(_take)/gather | solution.py:31
  1215.0 0.1 fusion.67
  1215.0 1.0 fusion.5
  1216.0 6.1 select_select_fusion
  1222.1 2.7 fusion.19
  1224.8 1.6 collective-permute-start.4
  1226.5 0.7 collective-permute-start.3
  1227.2 2.4 collective-permute-start.1
  1229.6 1.3 collective-permute-start.2
  1230.9 1.3 copy.62
  1232.2 2.5 fusion.58
  1234.7 2.5 copy.61
  1237.2 2.6 copy.60
  1239.8 2.5 copy.59
  1242.3 2.6 copy.58
  1244.9 1.3 copy.57
  1246.2 3.0 fusion.46
  1249.2 2.6 copy.56
  1251.8 2.6 copy.55
  1254.4 2.6 copy.54
  1257.0 2.5 copy.53
  1259.5 2.6 copy.52
  1262.1 2.6 copy.51
  1264.7 1.3 copy.50
  1266.0 2.6 copy.49
  1268.5 7.1 fusion.8
  1275.6 1.2 copy.46
  1276.9 2.0 copy.45
  1278.9 2.0 copy.43
  1281.0 2.1 copy.44
  1283.0 1.8 fusion.6
  1284.8 1.8 fusion.7
  1286.6 1.8 convolution_add_fusion.1
  1288.4 2.7 fusion.1
  1291.1 1.6 copy.47
  1292.7 2.1 fusion.11
  1294.8 0.2 copy.48
  1295.0 0.3 stack.2
  1295.3 57.3 %all_to_all.5 = bf16[8,256,1024]{1,2,0:T(8,128)(2,1)} all-to-all(bf16[8,256,1024]{1,2,0:T(8,128)(2,1)S(1)} %stack.2), channel_id=1, replica_groups=mesh['ctx'=16,'tp'=8] {'tp'}, dimensions={0} | all-to-all | bytes 8388608 | tf_op jit(solution)/shard_map/all_to_all | solution.py:68
  1352.5 12.4 convolution_convert_fusion
  (24 shorter events, 0.1 us)
Async XLA Ops:
  6.5 1346.0 %all-gather.2.cloned.1.call-start = ((), (), s32[]{:S(2)}) async-start(), calls=%async_computation.1 | async-start | bytes 17825792 | tf_op jit(solution)/shard_map/all_gather | solution.py:75
  7.4 1214.8 %collective-permute-start = (bf16[3,6,1024]{2,1,0:T(8,128)(2,1)S(1)}, bf16[3,6,1024]{2,1,0:T(8,128)(2,1)S(1)}, u32[]{:S(2)}, u32[]{:S(2)}) collective-permute-start(bf16[3,6,1024]{2,1,0:T(8,128)(2,1)S(1)} %slice.240), channel_id=1, source_target_pairs={{120,0},{0,8},{8,16},{16,24},{24,32},{32,40},{40,48},{48,56},{56,6... | collective-permute-start | bytes 110600 | tf_op jit(solution)/shard_map/ppermute | solution.py:11
  11.7 1.4 copy-start.5
  1154.9 60.1 %copy-start.4 = (f32[3,7,1024]{2,1,0:T(8,128)S(1)}, f32[3,7,1024]{2,1,0:T(8,128)}, u32[]{:S(2)}) copy-start(f32[3,7,1024]{2,1,0:T(8,128)} %param.6) | copy-start | bytes 258052
  1216.0 6.1 copy-start
  1224.8 50.8 %collective-permute-start.4 = (bf16[256,1024]{1,0:T(8,128)(2,1)}, bf16[256,1024]{1,0:T(8,128)(2,1)}, u32[]{:S(2)}, u32[]{:S(2)}) collective-permute-start(bf16[256,1024]{1,0:T(8,128)(2,1)} %get-tuple-element.5), channel_id=1, source_target_pairs={{96,0},{104,8},{112,16},{120,24},{0,32},{8,40},{16,48},{24,56},{32... | collective-permute-start | bytes 1572872 | tf_op jit(solution)/shard_map/ppermute | solution.py:11
  1226.5 50.4 %collective-permute-start.3 = (bf16[256,1024]{1,0:T(8,128)(2,1)}, bf16[256,1024]{1,0:T(8,128)(2,1)}, u32[]{:S(2)}, u32[]{:S(2)}) collective-permute-start(bf16[256,1024]{1,0:T(8,128)(2,1)} %get-tuple-element.5), channel_id=1, source_target_pairs={{104,0},{112,8},{120,16},{0,24},{8,32},{16,40},{24,48},{32,56},{40... | collective-permute-start | bytes 1572872 | tf_op jit(solution)/shard_map/ppermute | solution.py:11
  1227.2 51.7 %collective-permute-start.1 = (bf16[256,1024]{1,0:T(8,128)(2,1)}, bf16[256,1024]{1,0:T(8,128)(2,1)}, u32[]{:S(2)}, u32[]{:S(2)}) collective-permute-start(bf16[256,1024]{1,0:T(8,128)(2,1)} %get-tuple-element.5), channel_id=1, source_target_pairs={{120,0},{0,8},{8,16},{16,24},{24,32},{32,40},{40,48},{48,56},{56,6... | collective-permute-start | bytes 1572872 | tf_op jit(solution)/shard_map/ppermute | solution.py:11
  1229.6 51.4 %collective-permute-start.2 = (bf16[256,1024]{1,0:T(8,128)(2,1)}, bf16[256,1024]{1,0:T(8,128)(2,1)}, u32[]{:S(2)}, u32[]{:S(2)}) collective-permute-start(bf16[256,1024]{1,0:T(8,128)(2,1)} %get-tuple-element.5), channel_id=1, source_target_pairs={{112,0},{120,8},{0,16},{8,24},{16,32},{24,40},{32,48},{40,56},{48,... | collective-permute-start | bytes 1572872 | tf_op jit(solution)/shard_map/ppermute | solution.py:11
  1283.0 1.8 copy-start.1
  1284.8 1.8 copy-start.2
  1286.6 1.8 copy-start.3
  1291.1 1.6 copy-start.6
Sparse Core Ops, SparseCore 0:
  10.2 94.0 all-gather.1
